TPU v7x, 512 devices: a whole 4x8x8 slice. The times are simulated.
512 devices in a mesh: context: 8 (over z), expert: 32 (over x, y), dp: 2 (over core).
Axes of the slice: x: 4, y: 8, z: 8, core: 2. Of those that a mesh axis runs over, the one named last changes fastest.
Arguments:
- residual: bfloat16 [32768, 1024], P(('dp', 'expert', 'context')), parts along dimension 0, may hold values from -6 to 6
- queries: bfloat16 [32768, 2048], P(('dp', 'expert', 'context')), parts along dimension 0, may hold values from -4.6 to 4.6
- key_vectors: bfloat16 [32768, 256], P(('dp', 'expert', 'context')), parts along dimension 0, may hold values from -5 to 5
- value_vectors: bfloat16 [32768, 256], P(('dp', 'expert', 'context')), parts along dimension 0, may hold values from -5 to 5
- output_weight: bfloat16 [2048, 1024], P('context'), may hold values from -0.875 to 0.875
- norm_gain: float32 [1024], replicated, may hold values from 0.1 to 1.9
- routes: int32 [32768, 8], P(('dp', 'expert', 'context')), parts along dimension 0, may hold values from 0 to 127, all different within a row; in each aligned block of 64 rows (0 to 63, 64 to 127, ...) at most 5 rows name the same one
- gate_levels: int32 [32768, 8], P(('dp', 'expert', 'context')), parts along dimension 0, may hold values from 16 to 96
- expert_in: bfloat16 [256, 1024, 384], P(('context', 'expert')), may hold values from -0.1875 to 0.1875
- expert_out: bfloat16 [256, 192, 1024], P(('context', 'expert')), may hold values from -0.3125 to 0.3125
Outputs:
- layer_out: float32 [32768, 1024], P(('dp', 'expert', 'context')), parts along dimension 0
There are 2 independent parts, one for each index of `dp`. A program takes and returns all parts, laid end to end along the dimension named above; an argument that names none is the same for every part. Nothing has to cross between parts.
Inputs may be any that keep to these rules, and one draw needn't show every extreme that they name: `routes`: in the rows of one device no expert is named more than 5 times, and in every draw some expert reaches 5 in some device's rows; each row names 8 different experts.
All inputs are finite; a program needn't handle non-finite values.
Results may differ from a plain program's by a relative error of at most 0.022.
Values may be sent and summed in bfloat16 or wider, within the bound.
No kernel may reach another device: no remote copies, remote signals or barrier semaphores. Data moves between devices by JAX's collectives and lax.ppermute only.
A program may use at most 192 MiB of HBM per device.

v0:
```python
import math
import jax
import jax.numpy as jnp
import numpy as np
from jax import lax
from jax.sharding import PartitionSpec as P

HD = 128


def expert_apply(gathered, weight_in, weight_out):
    projection = jnp.dot(gathered, weight_in, preferred_element_type=jnp.float32)
    inner_half = weight_in.shape[1] // 2
    activated = (jax.nn.silu(projection[:, :inner_half]) * projection[:, inner_half:]).astype(
        jnp.bfloat16
    )
    return jnp.dot(activated, weight_out, preferred_element_type=jnp.float32).astype(jnp.bfloat16)


def local(
    residual,
    queries,
    key_vectors,
    value_vectors,
    output_weight,
    norm_gain,
    routes,
    gate_levels,
    expert_in,
    expert_out,
):
    context_size = lax.axis_size("context")
    expert_size = lax.axis_size("expert")
    tok_rows, width = residual.shape
    head_count = queries.shape[1] // HD
    key_head_count = key_vectors.shape[1] // HD
    group_size = head_count // key_head_count
    heads_here = head_count // context_size
    keys_here = max(1, heads_here // group_size)
    queries_per_key = min(heads_here, group_size)
    group_rows = tok_rows * context_size
    weight_in = expert_in[0]
    weight_out = expert_out[0]
    head_table = (
        (
            np.arange(context_size)[:, None] * heads_here // group_size
            + np.arange(keys_here)[None, :]
        )
        .reshape(-1)
        .astype(np.int32)
    )
    key_select = key_vectors.reshape(tok_rows, key_head_count, HD)[:, head_table].reshape(
        tok_rows, context_size * keys_here * HD
    )
    value_select = value_vectors.reshape(tok_rows, key_head_count, HD)[:, head_table].reshape(
        tok_rows, context_size * keys_here * HD
    )
    query_local, key_local, value_local = (
        lax.all_to_all(queries, "context", split_axis=1, concat_axis=0, tiled=True),
        lax.all_to_all(key_select, "context", split_axis=1, concat_axis=0, tiled=True),
        lax.all_to_all(value_select, "context", split_axis=1, concat_axis=0, tiled=True),
    )
    own_block = lax.axis_index("expert")
    scaling = 1.0 / math.sqrt(HD)
    to_count = query_local.shape[0]
    query_sets = [
        (
            query_local.reshape(to_count, keys_here, queries_per_key, HD)
            .transpose(1, 0, 2, 3)
            .reshape(keys_here, to_count * queries_per_key, HD),
            own_block * group_rows
            + jnp.arange(group_rows * queries_per_key, dtype=jnp.int32) // queries_per_key,
            (own_block + 1) * group_rows,
        )
    ]
    set_counts = [group_rows]
    initial = tuple(
        (
            (
                jnp.full((keys_here, count * queries_per_key), -1e30, jnp.float32),
                jnp.zeros((keys_here, count * queries_per_key), jnp.float32),
                jnp.zeros((keys_here, count * queries_per_key, HD), jnp.float32),
            )
            for count in set_counts
        )
    )
    start = jnp.int32(0)
    key_piece = lax.all_gather(key_local, "expert", axis=0, tiled=True)
    value_piece = lax.all_gather(value_local, "expert", axis=0, tiled=True)
    piece_rows = key_piece.shape[0]
    key_heads = key_piece.reshape(piece_rows, keys_here, HD).transpose(1, 0, 2)
    value_heads = value_piece.reshape(piece_rows, keys_here, HD).transpose(1, 0, 2)
    key_position = jnp.arange(piece_rows, dtype=jnp.int32)
    updated = []
    for query_set, state in zip(query_sets, initial):
        query_rows, query_position, key_limit = query_set

        def update(inner, query_rows=query_rows, query_position=query_position):
            run_max, run_total, accum = inner
            allowed = (key_position[None, :] <= query_position[:, None])[None]
            scores = (
                jnp.einsum(
                    "grd,gnd->grn", query_rows, key_heads, preferred_element_type=jnp.float32
                )
                * scaling
            )
            masked = jnp.where(allowed, scores, -1e30)
            new_max = jnp.maximum(run_max, jnp.max(masked, axis=2))
            weights = jnp.where(allowed, jnp.exp(masked - new_max[:, :, None]), 0.0)
            run_total = jnp.sum(weights, axis=2)
            accum = jnp.einsum(
                "grn,gnd->grd",
                weights.astype(jnp.bfloat16),
                value_heads,
                preferred_element_type=jnp.float32,
            )
            return (new_max, run_total, accum)

        def unchanged(inner):
            return inner

        updated.append(lax.cond(start < key_limit, update, unchanged, state))
    states = tuple(updated)
    run_max, run_total, accum = states[0]
    result = (accum / run_total[:, :, None]).astype(jnp.bfloat16)
    attention = (
        result.reshape(keys_here, group_rows, queries_per_key, HD)
        .transpose(1, 0, 2, 3)
        .reshape(group_rows, heads_here * HD)
    )
    projected = lax.psum_scatter(
        jnp.dot(attention, output_weight, preferred_element_type=jnp.float32).astype(jnp.bfloat16),
        "context",
        scatter_dimension=0,
        tiled=True,
    ).astype(jnp.float32)
    hidden_state = residual.astype(jnp.float32) + projected
    mean_square = jnp.mean(hidden_state * hidden_state, axis=1, keepdims=True)
    normed = (hidden_state * lax.rsqrt(mean_square + 1e-06) * norm_gain).astype(jnp.bfloat16)
    top_count = routes.shape[1]
    expert_count = expert_size * context_size // 2
    group_experts = expert_size // 2
    capacity = min(tok_rows, max(2, 5 * tok_rows * top_count // (4 * expert_count)))
    slot_count = expert_count * capacity
    flat_routes = routes.reshape(-1)
    expert_hits = (
        flat_routes[:, None] == jnp.arange(expert_count, dtype=jnp.int32)[None, :]
    ).astype(jnp.int32)
    earlier = jnp.cumsum(expert_hits, axis=0) - expert_hits
    target_slot = flat_routes * capacity + jnp.sum(earlier * expert_hits, axis=1)
    placement = (
        target_slot.reshape(tok_rows, top_count)[:, :, None]
        == jnp.arange(slot_count, dtype=jnp.int32)[None, None, :]
    )
    sending = jnp.any(placement, axis=1).astype(jnp.bfloat16)
    outgoing = lax.dot_general(
        sending, normed, (((0,), (0,)), ((), ())), preferred_element_type=jnp.float32
    ).astype(jnp.bfloat16)
    gate_shares = jnp.sum(
        jnp.where(placement, gate_levels[:, :, None].astype(jnp.float32) / 256.0, 0.0), axis=1
    ).astype(jnp.bfloat16)
    arrived = lax.all_to_all(
        outgoing.reshape(context_size, group_experts, capacity, width),
        "context",
        split_axis=0,
        concat_axis=0,
        tiled=True,
    )
    item_count = arrived.shape[2]
    copies = jnp.broadcast_to(
        arrived.transpose(1, 0, 2, 3)[:, None], (group_experts, 2, context_size, item_count, width)
    ).reshape(expert_size, context_size, item_count, width)
    rows_in = lax.all_to_all(copies, "expert", split_axis=0, concat_axis=0, tiled=True)
    partial_out = expert_apply(rows_in.reshape(-1, width), weight_in, weight_out).reshape(
        rows_in.shape
    )
    came_back = lax.all_to_all(partial_out, "expert", split_axis=0, concat_axis=0, tiled=True)
    summed = (
        came_back.reshape(group_experts, 2, context_size, item_count, width)
        .astype(jnp.float32)
        .sum(axis=1)
        .astype(jnp.bfloat16)
    )
    result = summed.transpose(1, 0, 2, 3)
    answers = lax.all_to_all(result, "context", split_axis=0, concat_axis=0, tiled=True)
    moe_sum = jnp.dot(
        gate_shares, answers.reshape(slot_count, width), preferred_element_type=jnp.float32
    )
    return hidden_state + moe_sum


def solution(mesh):
    return jax.shard_map(
        local,
        mesh=mesh,
        in_specs=(
            P(("dp", "expert", "context"), None),
            P(("dp", "expert", "context"), None),
            P(("dp", "expert", "context"), None),
            P(("dp", "expert", "context"), None),
            P("context", None),
            P(),
            P(("dp", "expert", "context"), None),
            P(("dp", "expert", "context"), None),
            P(("context", "expert"), None, None),
            P(("context", "expert"), None, None),
        ),
        out_specs=P(("dp", "expert", "context"), None),
        check_vma=False,
    )
```

profile of v0, /device:TPU:8, one launch (start us, length us, event | category | flops | bytes accessed | tf_op | source)
XLA Modules:
  0.0 555.0 jit_solution(13816407835851833400)
XLA Ops:
  6.5 0.7 pad_clamp_fusion
  7.3 0.8 copy_bitcast_fusion.2
  8.0 0.6 gather_fusion
  8.6 19.3 %all_to_all.68 = bf16[64,8,128]{2,0,1:T(8,128)(2,1)} all-to-all(bf16[64,8,128]{2,0,1:T(8,128)(2,1)S(1)} %bitcast.70), channel_id=1, replica_groups=mesh['context'=8,'expert'=32,'dp'=2] {'context'}, dimensions={1} | all-to-all | bytes 262144 | tf_op jit(solution)/shard_map/all_to_all | solution.py:60
  28.0 0.8 copy_bitcast_fusion.1
  28.8 0.6 gather_fusion.1
  29.3 12.1 %all_to_all.69 = bf16[64,8,128]{2,0,1:T(8,128)(2,1)} all-to-all(bf16[64,8,128]{2,0,1:T(8,128)(2,1)S(1)} %bitcast.69), channel_id=1, replica_groups=mesh['context'=8,'expert'=32,'dp'=2] {'context'}, dimensions={1} | all-to-all | bytes 262144 | tf_op jit(solution)/shard_map/all_to_all | solution.py:61
  41.5 1.7 copy.96
  43.2 3.4 all-to-all-start
  46.6 10.3 %all-to-all-done = bf16[64,8,256]{2,0,1:T(8,128)(2,1)S(1)} async-done(((bf16[64,8,256]{2,0,1:T(8,128)(2,1)}), bf16[64,8,256]{2,0,1:T(8,128)(2,1)S(1)}, u32[]{:S(2)}, u32[]{:S(2)}) %all-to-all-start) | async-done | bytes 262176 | tf_op jit(solution)/shard_map/all_to_all | solution.py:59
  57.0 54.5 %all-gather.3.cloned.1.call-done = bf16[16384,128]{1,0:T(8,128)(2,1)} async-done(((bf16[512,128]{1,0:T(8,128)(2,1)}), bf16[16384,128]{1,0:T(8,128)(2,1)}) %all-gather.3.cloned.1.call-update) | async-done | bytes 4194320 | tf_op jit(solution)/shard_map/all_gather | solution.py:88
  111.5 87.7 %all-gather.5.cloned.1.call-done = bf16[16384,128]{1,0:T(8,128)(2,1)} async-done(((bf16[512,128]{1,0:T(8,128)(2,1)}), bf16[16384,128]{1,0:T(8,128)(2,1)}) %all-gather.5.cloned.1.call-update) | async-done | bytes 4194320 | tf_op jit(solution)/shard_map/all_gather | solution.py:89
  199.3 74.4 %conditional.1 = (f32[1,1024]{1,0:T(1,128)S(1)}, f32[1,1024,128]{2,1,0:T(8,128)S(1)}) conditional(s32[]{:T(128)} %convert_element_type.51, () %tuple.19, (s32[16384]{0:T(1024)S(1)}, s32[]{:T(128)}, s32[1024]{0:T(1024)S(1)}, bf16[8,64,256]{2,1,0:T(8,128)(2,1)S(1)}, bf16[16384,128]{1,0:T(8,128)(2,1)}, /*index=5*/bf16[16384,128]{1,0:T(8,128)(2,1)}) %tuple.32), branch_computations={%region_0.1_spmd, %region_1.4_spmd} | conditional | flops 8858378240 | bytes 211267616 | solution.py:122
  199.3 0.1 reshape.111
  199.4 25.7 %fusion = (f32[1024]{0:T(1024)S(1)}, f32[1024,16384]{1,0:T(8,128)}) fusion(s32[16384]{0:T(1024)S(1)} %get-tuple-element.90, s32[1024]{0:T(1024)S(1)} %fusion.8, bf16[1024,128]{1,0:T(8,128)(2,1)S(1)} %reshape.111, bf16[16384,128]{1,0:T(8,128)(2,1)} %get-tuple-element.94), kind=kOutput, calls=%fused_computation.4 | convolution fusion | flops 4362075136 | bytes 71639040 | tf_op jit(solution)/shard_map/cond/branch_1_fun/grd,gnd->grn/dot_general | solution.py:102
  225.2 26.5 %fusion.5 = f32[1,1024,128]{2,1,0:T(8,128)S(1)} fusion(bf16[16384,128]{1,0:T(8,128)(2,1)} %get-tuple-element.95, f32[1024,16384]{1,0:T(8,128)} %get-tuple-element.113, f32[1024]{0:T(1024)S(1)} %broadcast_maximum_fusion, s32[16384]{0:T(1024)S(1)} %get-tuple-element.90, s32[1024]{0:T(1024)S(1)} %fusion.8), kind=kOutput, calls=%fused_computation.8 | convolution fusion | flops 4395630592 | bytes 71901184 | tf_op jit(solution)/shard_map/cond/branch_1_fun/grn,gnd->grd/dot_general | solution.py:111
  251.6 22.1 %fusion.2 = f32[1024]{0:T(1024)S(1)} fusion(f32[1024,16384]{1,0:T(8,128)} %get-tuple-element.113, f32[1024]{0:T(1024)S(1)} %broadcast_maximum_fusion, s32[16384]{0:T(1024)S(1)} %get-tuple-element.90, s32[1024]{0:T(1024)S(1)} %fusion.8), kind=kLoop, calls=%fused_computation.6 | loop fusion | flops 100662272 | bytes 67186688 | tf_op jit(solution)/shard_map/cond/branch_1_fun/reduce_sum | solution.py:110
  273.8 0.2 divide_convert_fusion
  274.1 1.4 convolution_convert_fusion.2
  275.6 0.1 eq.42
  275.8 0.1 copy.76
  275.9 0.2 fusion.22
  276.2 0.2 fusion.21
  276.7 0.5 fusion.13
  277.2 37.8 %reduce-scatter.2.cloned.1.call-done = bf16[64,1024]{1,0:T(8,128)(2,1)} async-done(((bf16[512,1024]{1,0:T(8,128)(2,1)}), bf16[64,1024]{1,0:T(8,128)(2,1)}) %reduce-scatter.2.cloned.1.call-update) | async-done | bytes 131088 | tf_op jit(solution)/shard_map/reduce_scatter | solution.py:131
  315.0 1.0 multiply_reduce_fusion
  316.1 2.5 convolution_convert_fusion.1
  318.7 2.6 reshape.124
  321.3 0.9 copy.81
  322.2 34.2 %all_to_all.70 = bf16[8,16,5,1024]{3,1,2,0:T(8,128)(2,1)S(1)} all-to-all(bf16[8,16,5,1024]{3,1,2,0:T(8,128)(2,1)S(1)} %copy.81), channel_id=1, replica_groups=mesh['context'=8,'expert'=32,'dp'=2] {'context'}, dimensions={0} | all-to-all | bytes 2621440 | tf_op jit(solution)/shard_map/all_to_all | solution.py:162
  356.4 0.7 copy.82
  357.1 0.3 broadcast_in_dim.54
  357.4 66.3 %all_to_all.71 = bf16[32,8,5,1024]{3,1,2,0:T(8,128)(2,1)S(1)} all-to-all(bf16[32,8,5,1024]{3,1,2,0:T(8,128)(2,1)S(1)} %bitcast.61), channel_id=1, replica_groups=mesh['context'=8,'expert'=32,'dp'=2] {'expert'}, dimensions={0} | all-to-all | bytes 5242880 | tf_op jit(solution)/shard_map/all_to_all | solution.py:173
  423.7 4.0 copy.83
  427.7 4.9 reshape.126
  432.7 1.3 fusion.15
  433.9 0.9 convolution_convert_fusion
  434.8 2.9 reshape.127
  437.7 4.9 copy.84
  442.6 61.2 %all_to_all.72 = bf16[32,8,5,1024]{3,1,2,0:T(8,128)(2,1)S(1)} all-to-all(bf16[32,8,5,1024]{3,1,2,0:T(8,128)(2,1)S(1)} %copy.84), channel_id=1, replica_groups=mesh['context'=8,'expert'=32,'dp'=2] {'expert'}, dimensions={0} | all-to-all | bytes 5242880 | tf_op jit(solution)/shard_map/all_to_all | solution.py:177
  503.8 0.6 bitcast_reduce_fusion
  504.4 1.8 copy.86
  506.2 6.4 %all-to-all-start.6 = ((bf16[8,16,5,1024]{3,1,2,0:T(8,128)(2,1)}), bf16[8,16,5,1024]{3,1,2,0:T(8,128)(2,1)}, u32[]{:S(2)}, u32[]{:S(2)}) async-start(bf16[8,16,5,1024]{3,1,2,0:T(8,128)(2,1)} %copy.86), calls=%async_computation.7 | async-start | bytes 2621440 | tf_op jit(solution)/shard_map/all_to_all | solution.py:185
  512.7 0.5 select_reduce_fusion
  513.2 29.2 %all-to-all-done.6 = bf16[8,16,5,1024]{3,1,2,0:T(8,128)(2,1)} async-done(((bf16[8,16,5,1024]{3,1,2,0:T(8,128)(2,1)}), bf16[8,16,5,1024]{3,1,2,0:T(8,128)(2,1)}, u32[]{:S(2)}, u32[]{:S(2)}) %all-to-all-start.6) | async-done | bytes 1310752 | tf_op jit(solution)/shard_map/all_to_all | solution.py:185
  542.4 2.2 copy.87
  544.6 1.4 reshape.129
  546.1 2.4 convolution_add_fusion
  (46 shorter events, 0.9 us)
Async XLA Ops:
  6.5 426.1 %copy-start = (bf16[1,1024,384]{2,1,0:T(8,128)(2,1)S(1)}, bf16[1,1024,384]{2,1,0:T(8,128)(2,1)}, u32[]{:S(2)}) copy-start(bf16[1,1024,384]{2,1,0:T(8,128)(2,1)} %param.23) | copy-start | bytes 2359300
  6.5 105.0 %all-gather.3.cloned.1.call-start = ((), (), s32[]{:S(2)}) async-start(), calls=%async_computation.8 | async-start | bytes 4325376 | tf_op jit(solution)/shard_map/all_gather | solution.py:88
  28.0 171.3 %all-gather.5.cloned.1.call-start = ((), (), s32[]{:S(2)}) async-start(), calls=%async_computation.9 | async-start | bytes 4325376 | tf_op jit(solution)/shard_map/all_gather | solution.py:89
  43.2 13.8 %all-to-all-start = ((bf16[64,8,256]{2,0,1:T(8,128)(2,1)}), bf16[64,8,256]{2,0,1:T(8,128)(2,1)S(1)}, u32[]{:S(2)}, u32[]{:S(2)}) async-start(bf16[64,8,256]{2,0,1:T(8,128)(2,1)} %bitcast.57), calls=%async_computation | async-start | bytes 524288 | tf_op jit(solution)/shard_map/all_to_all | solution.py:59
  46.6 268.4 %reduce-scatter.2.cloned.1.call-start = ((), (), s32[]{:S(2)}) async-start(), calls=%async_computation.10 | async-start | bytes 1179648 | tf_op jit(solution)/shard_map/reduce_scatter | solution.py:131
  199.3 74.8 %copy-start.3 = (bf16[256,1024]{1,0:T(8,128)(2,1)S(1)}, bf16[256,1024]{1,0:T(8,128)(2,1)}, u32[]{:S(2)}) copy-start(bf16[256,1024]{1,0:T(8,128)(2,1)} %param.19) | copy-start | bytes 1572868
  273.7 1.8 copy-start.6
  273.7 41.3 %copy-start.1 = (bf16[64,1024]{1,0:T(8,128)(2,1)S(1)}, bf16[64,1024]{1,0:T(8,128)(2,1)}, u32[]{:S(2)}) copy-start(bf16[64,1024]{1,0:T(8,128)(2,1)} %param.15) | copy-start | bytes 393220
  273.7 42.4 %copy-start.7 = (f32[1024]{0:T(1024)S(1)}, f32[1024]{0:T(1024)}, u32[]{:S(2)}) copy-start(f32[1024]{0:T(1024)} %param.20) | copy-start | bytes 12292
  276.7 39.4 %copy-start.4 = (s32[64,8]{1,0:T(8,128)}, s32[64,8]{1,0:T(8,128)S(1)}, u32[]{:S(2)}) copy-start(s32[64,8]{1,0:T(8,128)S(1)} %copy.79) | copy-start | bytes 6148
  432.6 1.3 copy-start.9
  503.8 8.8 %copy-start.8 = (s32[64,8]{0,1:T(8,128)S(1)}, s32[64,8]{0,1:T(8,128)}, u32[]{:S(2)}) copy-start(s32[64,8]{0,1:T(8,128)} %param.22) | copy-start | bytes 6148
  503.8 8.9 %copy-start.5 = (s32[64,8]{1,0:T(8,128)S(1)}, s32[64,8]{1,0:T(8,128)}, u32[]{:S(2)}) copy-start(s32[64,8]{1,0:T(8,128)} %copy-done.4) | copy-start | bytes 6148
  506.2 39.9 %copy-start.2 = (bf16[64,1024]{1,0:T(8,128)(2,1)S(1)}, bf16[64,1024]{1,0:T(8,128)(2,1)}, u32[]{:S(2)}) copy-start(bf16[64,1024]{1,0:T(8,128)(2,1)} %reduce-scatter.2.cloned.1.call-done) | copy-start | bytes 393220
  506.2 36.2 %all-to-all-start.6 = ((bf16[8,16,5,1024]{3,1,2,0:T(8,128)(2,1)}), bf16[8,16,5,1024]{3,1,2,0:T(8,128)(2,1)}, u32[]{:S(2)}, u32[]{:S(2)}) async-start(bf16[8,16,5,1024]{3,1,2,0:T(8,128)(2,1)} %copy.86), calls=%async_computation.7 | async-start | bytes 2621440 | tf_op jit(solution)/shard_map/all_to_all | solution.py:185
Sparse Core Ops, SparseCore 0:
  28.1 83.4 all-gather.2
  114.7 84.5 all-gather.4
  275.7 39.3 reduce-scatter.1
where the time goes:
time: 556 us; the launch traced here: 555 us
  waiting for transfers between devices  220 us (40%)
  blocking collectives  193 us (35%)
  matrix products  60.7 us (11%)
  local copies, waits for them, and re-layouts  32 us (6%)
  other arithmetic  26.1 us (5%)
  between operations  13.4 us (2%)
  starting transfers between devices  9.92 us (2%)
    all_gather x1, waiting for transfers between devices, local(): value_piece = lax.all_gather(value_local, 'expert', axis=0, tiled=True)  87.7 us
    all_to_all x1, blocking collectives, local(): lax.all_to_all(copies, 'expert', split_axis=0, concat_axis=0, tiled=True)  66.3 us
    all_to_all x1, blocking collectives, local(): lax.all_to_all(partial_out, 'expert', split_axis=0, concat_axis=0, tiled=...  61.2 us
    all_gather x1, waiting for transfers between devices, local(): key_piece = lax.all_gather(key_local, 'expert', axis=0, tiled=True)  54.5 us
    reduce_scatter x1, waiting for transfers between devices, local(): lax.psum_scatter(jnp.dot(attention, output_weight, preferred_element_type...  37.8 us
    all_to_all x1, blocking collectives, local(): lax.all_to_all(outgoing.reshape(context_size, group_experts, capacity, wi...  34.2 us
    all_to_all x1, waiting for transfers between devices, local(): lax.all_to_all(result, 'context', split_axis=0, concat_axis=0, tiled=True)  29.2 us
    dot_general x1, matrix products, update(): jnp.einsum('grn,gnd->grd', weights.astype(jnp.bfloat16), value_heads, pre...  26.5 us
  transfers between devices with their start and end apart: 5, of which 5 were waited for; matrix products, arithmetic and copies ran while one was open for 1% of the time, Pallas kernels for 0%

commit v1 on v0

--- a/solution.py
+++ b/solution.py
@@ -56,7 +56,12 @@
         tok_rows, context_size * keys_here * HD
     )
     query_local, key_local, value_local = (
-        lax.all_to_all(queries, "context", split_axis=1, concat_axis=0, tiled=True),
+        jnp.concatenate(
+            lax.all_to_all(
+                jnp.stack(jnp.split(queries, lax.axis_size("context"), axis=1)), "context", 0, 0
+            ),
+            axis=0,
+        ),
         lax.all_to_all(key_select, "context", split_axis=1, concat_axis=0, tiled=True),
         lax.all_to_all(value_select, "context", split_axis=1, concat_axis=0, tiled=True),
     )

time: 556 us -> 556 us (level)
  waiting for transfers between devices: 220 us -> 210 us
  local copies, waits for them, and re-layouts: 32 us -> 41.3 us
    unnamed x22 -> x29, local copies, waits for them, and re-layouts: 0.14 us -> 9.76 us
    all_gather x1, waiting for transfers between devices: 54.5 us -> 45.1 us  [local(): key_piece = lax.all_gather(key_local, 'expert', axis=0, tiled=True)]
  transfers between devices with their start and end apart: 5 -> 5, of which waited for: 5 -> 5; matrix products, arithmetic and copies ran while one was open for 1% -> 3% of each run, Pallas kernels for 0% -> 0%
where the time goes in v1:
time: 556 us; the launch traced here: 554 us
  waiting for transfers between devices  210 us (38%)
  blocking collectives  193 us (35%)
  matrix products  60.7 us (11%)
  local copies, waits for them, and re-layouts  41.3 us (7%)
  other arithmetic  26.1 us (5%)
  between operations  13.4 us (2%)
  starting transfers between devices  9.51 us (2%)
    all_gather x1, waiting for transfers between devices, local(): value_piece = lax.all_gather(value_local, 'expert', axis=0, tiled=True)  87.7 us
    all_to_all x1, blocking collectives, local(): lax.all_to_all(copies, 'expert', split_axis=0, concat_axis=0, tiled=True)  66.3 us
    all_to_all x1, blocking collectives, local(): lax.all_to_all(partial_out, 'expert', split_axis=0, concat_axis=0, tiled=...  61.1 us
    all_gather x1, waiting for transfers between devices, local(): key_piece = lax.all_gather(key_local, 'expert', axis=0, tiled=True)  45.1 us
    reduce_scatter x1, waiting for transfers between devices, local(): lax.psum_scatter(jnp.dot(attention, output_weight, preferred_element_type...  38 us
    all_to_all x1, blocking collectives, local(): lax.all_to_all(outgoing.reshape(context_size, group_experts, capacity, wi...  34.1 us
    all_to_all x1, waiting for transfers between devices, local(): lax.all_to_all(result, 'context', split_axis=0, concat_axis=0, tiled=True)  28.9 us
    dot_general x1, matrix products, update(): jnp.einsum('grn,gnd->grd', weights.astype(jnp.bfloat16), value_heads, pre...  26.5 us
  transfers between devices with their start and end apart: 5, of which 5 were waited for; matrix products, arithmetic and copies ran while one was open for 3% of the time, Pallas kernels for 0%

profile of v1, /device:TPU:8, one launch (start us, length us, event | category | flops | bytes accessed | tf_op | source)
XLA Modules:
  0.0 554.1 jit_solution(5412524585814898275)
XLA Ops:
  6.5 0.7 pad_clamp_fusion
  7.3 0.8 copy_bitcast_fusion.1
  8.0 0.6 gather_fusion
  8.6 19.3 %all_to_all.57 = bf16[64,8,128]{2,0,1:T(8,128)(2,1)} all-to-all(bf16[64,8,128]{2,0,1:T(8,128)(2,1)S(1)} %bitcast.80), channel_id=1, replica_groups=mesh['context'=8,'expert'=32,'dp'=2] {'context'}, dimensions={1} | all-to-all | bytes 262144 | tf_op jit(solution)/shard_map/all_to_all | solution.py:65
  28.0 0.8 copy_bitcast_fusion
  28.8 0.6 gather_fusion.1
  29.3 12.1 %all_to_all.58 = bf16[64,8,128]{2,0,1:T(8,128)(2,1)} all-to-all(bf16[64,8,128]{2,0,1:T(8,128)(2,1)S(1)} %bitcast.79), channel_id=1, replica_groups=mesh['context'=8,'expert'=32,'dp'=2] {'context'}, dimensions={1} | all-to-all | bytes 262144 | tf_op jit(solution)/shard_map/all_to_all | solution.py:66
  41.5 1.4 bitcast_dynamic-update-slice_fusion.7
  42.9 1.4 bitcast_dynamic-update-slice_fusion.6
  44.3 1.4 bitcast_dynamic-update-slice_fusion.5
  45.6 1.4 bitcast_dynamic-update-slice_fusion.4
  47.0 1.4 bitcast_dynamic-update-slice_fusion.3
  48.4 1.4 bitcast_dynamic-update-slice_fusion.2
  49.8 1.4 bitcast_dynamic-update-slice_fusion.1
  51.1 1.4 bitcast_dynamic-update-slice_fusion
  52.5 3.4 all-to-all-start
  56.0 10.3 %all-to-all-done = bf16[8,64,256]{2,1,0:T(8,128)(2,1)S(1)} async-done(((bf16[8,64,256]{2,1,0:T(8,128)(2,1)}), bf16[8,64,256]{2,1,0:T(8,128)(2,1)S(1)}, u32[]{:S(2)}, u32[]{:S(2)}) %all-to-all-start) | async-done | bytes 262176 | tf_op jit(solution)/shard_map/all_to_all | solution.py:60
  66.3 45.1 %all-gather.3.cloned.1.call-done = bf16[16384,128]{1,0:T(8,128)(2,1)} async-done(((bf16[512,128]{1,0:T(8,128)(2,1)}), bf16[16384,128]{1,0:T(8,128)(2,1)}) %all-gather.3.cloned.1.call-update) | async-done | bytes 4194320 | tf_op jit(solution)/shard_map/all_gather | solution.py:93
  111.5 87.7 %all-gather.5.cloned.1.call-done = bf16[16384,128]{1,0:T(8,128)(2,1)} async-done(((bf16[512,128]{1,0:T(8,128)(2,1)}), bf16[16384,128]{1,0:T(8,128)(2,1)}) %all-gather.5.cloned.1.call-update) | async-done | bytes 4194320 | tf_op jit(solution)/shard_map/all_gather | solution.py:94
  199.2 74.4 %conditional.1 = (f32[1,1024]{1,0:T(1,128)S(1)}, f32[1,1024,128]{2,1,0:T(8,128)S(1)}) conditional(s32[]{:T(128)} %convert_element_type.51, () %tuple.19, (s32[16384]{0:T(1024)S(1)}, s32[]{:T(128)}, s32[1024]{0:T(1024)S(1)}, bf16[8,64,256]{2,1,0:T(8,128)(2,1)S(1)}, bf16[16384,128]{1,0:T(8,128)(2,1)}, /*index=5*/bf16[16384,128]{1,0:T(8,128)(2,1)}) %tuple.20), branch_computations={%region_0.1_spmd, %region_1.4_spmd} | conditional | flops 8858378240 | bytes 211267616 | solution.py:127
  199.3 25.7 %fusion = (f32[1024]{0:T(1024)S(1)}, f32[1024,16384]{1,0:T(8,128)}) fusion(s32[16384]{0:T(1024)S(1)} %get-tuple-element.90, s32[1024]{0:T(1024)S(1)} %fusion.8, bf16[1024,128]{1,0:T(8,128)(2,1)S(1)} %reshape.107, bf16[16384,128]{1,0:T(8,128)(2,1)} %get-tuple-element.94), kind=kOutput, calls=%fused_computation.4 | convolution fusion | flops 4362075136 | bytes 71639040 | tf_op jit(solution)/shard_map/cond/branch_1_fun/grd,gnd->grn/dot_general | solution.py:107
  225.0 26.5 %fusion.5 = f32[1,1024,128]{2,1,0:T(8,128)S(1)} fusion(bf16[16384,128]{1,0:T(8,128)(2,1)} %get-tuple-element.95, f32[1024,16384]{1,0:T(8,128)} %get-tuple-element.101, f32[1024]{0:T(1024)S(1)} %broadcast_maximum_fusion, s32[16384]{0:T(1024)S(1)} %get-tuple-element.90, s32[1024]{0:T(1024)S(1)} %fusion.8), kind=kOutput, calls=%fused_computation.8 | convolution fusion | flops 4395630592 | bytes 71901184 | tf_op jit(solution)/shard_map/cond/branch_1_fun/grn,gnd->grd/dot_general | solution.py:116
  251.5 22.1 %fusion.2 = f32[1024]{0:T(1024)S(1)} fusion(f32[1024,16384]{1,0:T(8,128)} %get-tuple-element.101, f32[1024]{0:T(1024)S(1)} %broadcast_maximum_fusion, s32[16384]{0:T(1024)S(1)} %get-tuple-element.90, s32[1024]{0:T(1024)S(1)} %fusion.8), kind=kLoop, calls=%fused_computation.6 | loop fusion | flops 100662272 | bytes 67186688 | tf_op jit(solution)/shard_map/cond/branch_1_fun/reduce_sum | solution.py:115
  273.9 1.4 convolution_convert_fusion.2
  276.6 0.5 fusion.13
  277.1 38.0 %reduce-scatter.2.cloned.1.call-done = bf16[64,1024]{1,0:T(8,128)(2,1)} async-done(((bf16[512,1024]{1,0:T(8,128)(2,1)}), bf16[64,1024]{1,0:T(8,128)(2,1)}) %reduce-scatter.2.cloned.1.call-update) | async-done | bytes 131088 | tf_op jit(solution)/shard_map/reduce_scatter | solution.py:136
  315.0 1.0 multiply_reduce_fusion
  316.1 2.5 convolution_convert_fusion.1
  318.7 2.6 reshape.120
  321.3 0.9 copy.76
  322.2 34.1 %all_to_all.59 = bf16[8,16,5,1024]{3,1,2,0:T(8,128)(2,1)S(1)} all-to-all(bf16[8,16,5,1024]{3,1,2,0:T(8,128)(2,1)S(1)} %copy.76), channel_id=1, replica_groups=mesh['context'=8,'expert'=32,'dp'=2] {'context'}, dimensions={0} | all-to-all | bytes 2621440 | tf_op jit(solution)/shard_map/all_to_all | solution.py:167
  356.3 0.7 copy.77
  357.4 66.3 %all_to_all.60 = bf16[32,8,5,1024]{3,1,2,0:T(8,128)(2,1)S(1)} all-to-all(bf16[32,8,5,1024]{3,1,2,0:T(8,128)(2,1)S(1)} %bitcast.72), channel_id=1, replica_groups=mesh['context'=8,'expert'=32,'dp'=2] {'expert'}, dimensions={0} | all-to-all | bytes 5242880 | tf_op jit(solution)/shard_map/all_to_all | solution.py:178
  423.6 4.0 copy.78
  427.6 4.9 reshape.122
  432.6 1.3 fusion.15
  433.8 0.9 convolution_convert_fusion
  434.8 2.9 reshape.123
  437.6 4.9 copy.79
  442.5 61.1 %all_to_all.61 = bf16[32,8,5,1024]{3,1,2,0:T(8,128)(2,1)S(1)} all-to-all(bf16[32,8,5,1024]{3,1,2,0:T(8,128)(2,1)S(1)} %copy.79), channel_id=1, replica_groups=mesh['context'=8,'expert'=32,'dp'=2] {'expert'}, dimensions={0} | all-to-all | bytes 5242880 | tf_op jit(solution)/shard_map/all_to_all | solution.py:182
  503.6 0.6 bitcast_reduce_fusion
  504.2 1.8 copy.81
  506.1 6.0 %all-to-all-start.6 = ((bf16[8,16,5,1024]{3,1,2,0:T(8,128)(2,1)}), bf16[8,16,5,1024]{3,1,2,0:T(8,128)(2,1)}, u32[]{:S(2)}, u32[]{:S(2)}) async-start(bf16[8,16,5,1024]{3,1,2,0:T(8,128)(2,1)} %copy.81), calls=%async_computation.7 | async-start | bytes 2621440 | tf_op jit(solution)/shard_map/all_to_all | solution.py:190
  512.2 0.5 select_reduce_fusion
  512.7 28.9 %all-to-all-done.6 = bf16[8,16,5,1024]{3,1,2,0:T(8,128)(2,1)} async-done(((bf16[8,16,5,1024]{3,1,2,0:T(8,128)(2,1)}), bf16[8,16,5,1024]{3,1,2,0:T(8,128)(2,1)}, u32[]{:S(2)}, u32[]{:S(2)}) %all-to-all-start.6) | async-done | bytes 1310752 | tf_op jit(solution)/shard_map/all_to_all | solution.py:190
  541.6 2.2 copy.82
  543.8 1.4 reshape.125
  545.2 2.4 convolution_add_fusion
  (53 shorter events, 2.2 us)
Async XLA Ops:
  6.5 426.0 %copy-start = (bf16[1,1024,384]{2,1,0:T(8,128)(2,1)S(1)}, bf16[1,1024,384]{2,1,0:T(8,128)(2,1)}, u32[]{:S(2)}) copy-start(bf16[1,1024,384]{2,1,0:T(8,128)(2,1)} %param.23) | copy-start | bytes 2359300
  6.5 104.9 %all-gather.3.cloned.1.call-start = ((), (), s32[]{:S(2)}) async-start(), calls=%async_computation.8 | async-start | bytes 4325376 | tf_op jit(solution)/shard_map/all_gather | solution.py:93
  28.0 171.2 %all-gather.5.cloned.1.call-start = ((), (), s32[]{:S(2)}) async-start(), calls=%async_computation.9 | async-start | bytes 4325376 | tf_op jit(solution)/shard_map/all_gather | solution.py:94
  52.5 13.8 %all-to-all-start = ((bf16[8,64,256]{2,1,0:T(8,128)(2,1)}), bf16[8,64,256]{2,1,0:T(8,128)(2,1)S(1)}, u32[]{:S(2)}, u32[]{:S(2)}) async-start(bf16[8,64,256]{2,1,0:T(8,128)(2,1)} %bitcast_dynamic-update-slice_fusion), calls=%async_computation | async-start | bytes 524288 | tf_op jit(solution)/shard_map/all_to_all | solution.py:60
  55.9 259.1 %reduce-scatter.2.cloned.1.call-start = ((), (), s32[]{:S(2)}) async-start(), calls=%async_computation.10 | async-start | bytes 1179648 | tf_op jit(solution)/shard_map/reduce_scatter | solution.py:136
  199.2 74.7 %copy-start.3 = (bf16[256,1024]{1,0:T(8,128)(2,1)S(1)}, bf16[256,1024]{1,0:T(8,128)(2,1)}, u32[]{:S(2)}) copy-start(bf16[256,1024]{1,0:T(8,128)(2,1)} %param.19) | copy-start | bytes 1572868
  273.6 1.8 copy-start.6
  273.6 41.4 %copy-start.1 = (bf16[64,1024]{1,0:T(8,128)(2,1)S(1)}, bf16[64,1024]{1,0:T(8,128)(2,1)}, u32[]{:S(2)}) copy-start(bf16[64,1024]{1,0:T(8,128)(2,1)} %param.15) | copy-start | bytes 393220
  273.6 42.5 %copy-start.7 = (f32[1024]{0:T(1024)S(1)}, f32[1024]{0:T(1024)}, u32[]{:S(2)}) copy-start(f32[1024]{0:T(1024)} %param.20) | copy-start | bytes 12292
  276.6 39.5 %copy-start.4 = (s32[64,8]{1,0:T(8,128)}, s32[64,8]{1,0:T(8,128)S(1)}, u32[]{:S(2)}) copy-start(s32[64,8]{1,0:T(8,128)S(1)} %copy.74) | copy-start | bytes 6148
  432.6 1.3 copy-start.9
  503.6 8.4 %copy-start.8 = (s32[64,8]{0,1:T(8,128)S(1)}, s32[64,8]{0,1:T(8,128)}, u32[]{:S(2)}) copy-start(s32[64,8]{0,1:T(8,128)} %param.22) | copy-start | bytes 6148
  503.6 8.5 %copy-start.5 = (s32[64,8]{1,0:T(8,128)S(1)}, s32[64,8]{1,0:T(8,128)}, u32[]{:S(2)}) copy-start(s32[64,8]{1,0:T(8,128)} %copy-done.4) | copy-start | bytes 6148
  506.0 39.2 %copy-start.2 = (bf16[64,1024]{1,0:T(8,128)(2,1)S(1)}, bf16[64,1024]{1,0:T(8,128)(2,1)}, u32[]{:S(2)}) copy-start(bf16[64,1024]{1,0:T(8,128)(2,1)} %reduce-scatter.2.cloned.1.call-done) | copy-start | bytes 393220
  506.1 35.5 %all-to-all-start.6 = ((bf16[8,16,5,1024]{3,1,2,0:T(8,128)(2,1)}), bf16[8,16,5,1024]{3,1,2,0:T(8,128)(2,1)}, u32[]{:S(2)}, u32[]{:S(2)}) async-start(bf16[8,16,5,1024]{3,1,2,0:T(8,128)(2,1)} %copy.81), calls=%async_computation.7 | async-start | bytes 2621440 | tf_op jit(solution)/shard_map/all_to_all | solution.py:190
Sparse Core Ops, SparseCore 0:
  28.1 83.3 all-gather.2
  114.6 84.5 all-gather.4
  275.5 39.4 reduce-scatter.1
